TPU v7x, 768 devices: a whole 4x8x12 slice. The times are simulated.
768 devices in a mesh: grp: 8 (over y_hi, core), tp: 8 (over y_lo, x), seq: 12 (over z).
Axes of the slice: x: 4, y: 8 (y_hi: 4, y_lo: 2; y = y_hi * 2 + y_lo), z: 12, core: 2. Of those that a mesh axis runs over, the one named last changes fastest.
Arguments:
- crops: bfloat16 [8, 12, 576, 1024], P('grp', 'seq', 'tp'), may hold values from -6 to 6
- dout: bfloat16 [8, 12, 576, 1024], P('grp', 'seq', None, 'tp'), may hold values from -0.796875 to 0.796875
- crop_count: int32 [8], P('grp'), may hold values from 4 to 12, as said below
- crop_ids: int32 [8, 12], P('grp'), may hold values from 0 to 11, each once within a row
- seq_slot: int32 [8, 12], P('grp'), may hold values from 0 to 11, as said below
- norm_gain: bfloat16 [1024], replicated, may hold values from 0.099609375 to 1.8984375
- qkv_weight: bfloat16 [3, 1024, 1024], P(None, None, 'tp'), may hold values from -40 to 40
Outputs:
- weight_grad: float32 [3072, 1024], P(('grp', 'seq'), 'tp')
Inputs may be any that keep to these rules, and one draw needn't show every extreme that they name: `crop_count`: some page selects 12 crops. `seq_slot`: distinct within a row; only the first crop_count entries of a row are used. `crop_ids`: only the first crop_count entries of a row are used.
All inputs are finite; a program needn't handle non-finite values.
Results may differ from a plain program's by a relative error of at most 0.0084.
Values may be sent and summed in bfloat16 or wider, within the bound.
No kernel may reach another device: no remote copies, remote signals or barrier semaphores. Data moves between devices by JAX's collectives and lax.ppermute only.
A program may use at most 32 MiB of HBM per device.

v0:
```python
import jax
import jax.numpy as jnp
from jax import lax
from jax.experimental import pallas as pl
from jax.experimental.pallas import tpu as pltpu
from jax.sharding import Mesh, PartitionSpec as P


HD = 64
GRP_OUTER = 4
GRP_INNER = 2
TP_OUTER = 2
KERNEL_VMEM = 28 << 20

NN = (((1,), (0,)), ((), ()))
NT = (((1,), (1,)), ((), ()))
VMEM = pl.BlockSpec(memory_space=pltpu.VMEM)
SMEM = pl.BlockSpec(memory_space=pltpu.SMEM)


def near(value):
    return pltpu.with_memory_space_constraint(value, pltpu.VMEM)


def dot(a, b, dims=NN):
    return lax.dot_general(a, b, dims, preferred_element_type=jnp.float32)


def norm_kernel(inputs_ref, gain_ref, out_ref):
    values = inputs_ref[...].astype(jnp.float32)
    centred = values - jnp.mean(values, axis=-1, keepdims=True)
    spread = jnp.mean(centred * centred, axis=-1, keepdims=True)
    normed = centred * lax.rsqrt(spread + 1e-05) * gain_ref[...].astype(jnp.float32)
    out_ref[...] = normed.astype(jnp.bfloat16)


def layer_norm(inputs, gain):
    return pl.pallas_call(
        norm_kernel,
        out_shape=jax.ShapeDtypeStruct(inputs.shape, jnp.bfloat16),
        in_specs=[VMEM, VMEM],
        out_specs=VMEM,
        name="norm",
    )(inputs, gain)


def route_kernel(count_ref, ids_ref, slot_ref, pieces_ref, out_ref):
    out_ref[...] = jnp.zeros(out_ref.shape, out_ref.dtype)
    for rank in range(out_ref.shape[0]):

        @pl.when(rank < count_ref[0])
        def _():
            out_ref[ids_ref[0, rank]] = pieces_ref[slot_ref[0, rank]]


def by_candidate(count, ids, slots, pieces):
    return pl.pallas_call(
        route_kernel,
        out_shape=pltpu.VMEM(pieces.shape, pieces.dtype),
        in_specs=[SMEM, SMEM, SMEM, VMEM],
        out_specs=VMEM,
        name="route",
    )(count, ids, slots, pieces)


def grads_kernel(place_ref, *refs):
    *block_refs, weight_ref, cotangent_ref, theirs_ref, mine_ref, sums_ref = refs
    low = jnp.bfloat16
    both = block_refs[0].shape[0]
    part = both // TP_OUTER
    blocks = [ref[...] for ref in block_refs]
    normed = jnp.concatenate(
        [block[i * part : (i + 1) * part] for i in range(TP_OUTER) for block in blocks], 0
    )
    tok_count, width = normed.shape
    head_cols = cotangent_ref.shape[1]
    queries = dot(normed, weight_ref[0]).astype(low)
    key_rows = dot(normed, weight_ref[1]).astype(low)
    value_rows = dot(normed, weight_ref[2]).astype(low)
    half = tok_count // TP_OUTER
    first = place_ref[1] * part
    turn = jnp.where(first == 0, 0, half - first)
    upstream = cotangent_ref[...].astype(jnp.float32)
    upstream = jnp.concatenate(
        [pltpu.roll(upstream[i * half : (i + 1) * half], turn, 0) for i in range(TP_OUTER)], 0
    ).astype(low)
    head_of = lax.broadcasted_iota(jnp.int32, (tok_count, head_cols), 1) // HD
    zero = jnp.zeros((), low)
    score_scale = HD ** (-0.5)
    keys_t = key_rows.T
    grad_values, grad_keys, grad_queries = [], [], []
    for head in range(head_cols // HD):
        q = jnp.where(head_of == head, queries, zero)
        g = jnp.where(head_of == head, upstream, zero)
        scores = dot(key_rows, q, NT) * score_scale
        weights = jnp.exp(scores - jnp.max(scores, axis=0, keepdims=True))
        attention = weights / jnp.sum(weights, axis=0, keepdims=True)
        grad_attention = dot(value_rows, g, NT)
        mean = jnp.sum(attention * grad_attention, axis=0, keepdims=True)
        scaled = (attention * (grad_attention - mean) * score_scale).astype(low)
        grad_values.append(dot(attention.astype(low), g))
        grad_keys.append(dot(scaled, q))
        grad_queries.append(dot(keys_t[head * HD : (head + 1) * HD], scaled))
    normed_t = normed.T
    joined = (
        jnp.concatenate(grad_queries, 0).astype(low).T,
        sum(grad_keys).astype(low),
        sum(grad_values).astype(low),
    )
    for c, grad in enumerate(joined):
        sums_ref[pl.ds(c * width, width), :] = dot(normed_t, grad)
    core = place_ref[0]
    rows = theirs_ref.shape[1]
    for outer in range(GRP_OUTER):
        own = pl.multiple_of((outer * GRP_INNER + core) * rows, rows)
        other = pl.multiple_of((outer * GRP_INNER + 1 - core) * rows, rows)
        mine_ref[outer] = sums_ref[pl.ds(own, rows), :]
        theirs_ref[outer] = sums_ref[pl.ds(other, rows), :].astype(low)


def weight_partials(place, normed, weight, cotangent):
    width, head_cols = weight.shape[1:]
    half = (GRP_OUTER, 3 * width // (GRP_OUTER * GRP_INNER), head_cols)
    return pl.pallas_call(
        grads_kernel,
        out_shape=(
            pltpu.VMEM(half, jnp.bfloat16),
            pltpu.VMEM(half, jnp.float32),
        ),
        in_specs=[SMEM, *[VMEM] * len(normed), VMEM, VMEM],
        out_specs=(VMEM, VMEM),
        scratch_shapes=[pltpu.VMEM((3 * width, head_cols), jnp.float32)],
        compiler_params=pltpu.CompilerParams(vmem_limit_bytes=KERNEL_VMEM),
        name="grads",
    )(place, *normed, weight, cotangent)


def make_body(seq_size):
    def body(crops, dout, crop_count, crop_ids, seq_slot, norm_gain, qkv_weight):
        return step(crops, dout, crop_count, crop_ids, seq_slot, norm_gain, qkv_weight)

    def step(crops, dout, crop_count, crop_ids, seq_slot, norm_gain, qkv_weight):
        tok_local, _ = crops.shape[2:]
        tok_count, head_cols = dout.shape[2:]
        tp_inner = tok_count // tok_local // TP_OUTER
        chunk = tok_count // seq_size

        pieces = lax.all_to_all(
            dout[0, 0].reshape(seq_size, chunk, head_cols), "z", 0, 0, tiled=True
        )
        routed = by_candidate(crop_count, crop_ids, seq_slot, near(pieces))
        cotangent = lax.all_to_all(routed, "z", 0, 0, tiled=True)
        cotangent = cotangent.reshape(tok_count, head_cols)

        local = layer_norm(crops[0, 0], norm_gain[None])
        both = lax.all_gather(local, "yl", axis=0, tiled=True)
        normed = [near(both)]
        for d in range(1, tp_inner):
            pairs = [(i, (i - d) % tp_inner) for i in range(tp_inner)]
            normed.append(near(lax.ppermute(both, "x", pairs)))

        place = jnp.stack([lax.axis_index("core"), lax.axis_index("x")])
        theirs, mine = weight_partials(place, normed, near(qkv_weight), near(cotangent))

        received = lax.ppermute(theirs, "core", [(0, 1), (1, 0)])
        total = (mine + received.astype(jnp.float32)).astype(jnp.bfloat16)
        total = total.reshape(GRP_OUTER * seq_size, -1, head_cols)
        parts = lax.all_to_all(total, ("yh", "z"), 0, 0, tiled=True)
        return jnp.sum(parts.astype(jnp.float32), axis=0)

    return body


def solution(mesh):
    seq_size = mesh.shape["seq"]
    tp_inner = mesh.shape["tp"] // TP_OUTER
    fine = Mesh(
        mesh.devices.reshape(GRP_OUTER, GRP_INNER, TP_OUTER, tp_inner, seq_size),
        ("yh", "core", "yl", "x", "z"),
    )
    grp, tp = ("yh", "core"), ("yl", "x")
    in_specs = (
        P(grp, "z", tp, None),
        P(grp, "z", None, tp),
        P(grp),
        P(grp, None),
        P(grp, None),
        P(),
        P(None, None, tp),
    )
    out_specs = P((*grp, "z"), tp)
    return jax.shard_map(
        make_body(seq_size), mesh=fine, in_specs=in_specs, out_specs=out_specs, check_vma=False
    )
```

profile of v0, /device:TPU:2, one launch (start us, length us, event | category | flops | bytes accessed | tf_op | source)
XLA Modules:
  0.0 109.5 jit_solution(8130596280227121630)
XLA Ops:
  0.0 0.0 copy-start
  0.0 15.3 %all-to-all-start = ((bf16[12,48,128]{2,1,0:T(8,128)(2,1)}), bf16[12,48,128]{2,1,0:T(8,128)(2,1)S(1)}, u32[]{:S(2)}, u32[]{:S(2)}) async-start(bf16[12,48,128]{2,1,0:T(8,128)(2,1)} %bitcast.8), calls=%async_computation | async-start | bytes 294912 | tf_op jit(solution)/shard_map/all_to_all | solution.py:148
  15.9 12.2 %all-to-all-done.pieces_ref = bf16[12,48,128]{2,1,0:T(8,128)(2,1)S(1)} async-done(((bf16[12,48,128]{2,1,0:T(8,128)(2,1)}), bf16[12,48,128]{2,1,0:T(8,128)(2,1)S(1)}, u32[]{:S(2)}, u32[]{:S(2)}) %all-to-all-start) | async-done | bytes 147488 | tf_op jit(solution)/shard_map/all_to_all | solution.py:148
  28.1 1.4 %route.1 = bf16[12,48,128]{2,1,0:T(8,128)(2,1)} custom-call(s32[1]{0:T(128)S(6)} %copy.8.count_ref, s32[1,12]{1,0:T(1,128)} %ids_ref.1, s32[1,12]{1,0:T(1,128)} %slot_ref.1, bf16[12,48,128]{2,1,0:T(8,128)(2,1)S(1)} %all-to-all-done.pieces_ref), custom_call_target="tpu_custom_call" | custom-call | tf_op jit(solution)/shard_map/route/pallas_call | solution.py:57
  29.6 0.0 copy-start.1
  29.6 3.6 %all-to-all-start.1 = ((bf16[12,48,128]{2,1,0:T(8,128)(2,1)}), bf16[12,48,128]{2,1,0:T(8,128)(2,1)S(1)}, u32[]{:S(2)}, u32[]{:S(2)}) async-start(bf16[12,48,128]{2,1,0:T(8,128)(2,1)} %route.1), calls=%async_computation.1 | async-start | bytes 294912 | tf_op jit(solution)/shard_map/all_to_all | solution.py:152
  33.2 0.0 copy-done.1
  33.3 0.6 broadcast_in_dim.3.gain_ref
  33.9 1.8 %norm.1 = bf16[72,1024]{1,0:T(8,128)(2,1)} custom-call(bf16[72,1024]{1,0:T(8,128)(2,1)} %bitcast.9, bf16[1,1024]{1,0:T(2,128)(2,1)} %broadcast_in_dim.3.gain_ref), custom_call_target="tpu_custom_call" | custom-call | tf_op jit(solution)/shard_map/norm/pallas_call | solution.py:38
  35.7 6.0 %all_gather.3.refs_0_ = bf16[144,1024]{1,0:T(8,128)(2,1)S(1)} all-gather(bf16[72,1024]{1,0:T(8,128)(2,1)} %norm.1), channel_id=1, replica_groups=mesh['yh'=4,'core'=2,'yl'=2,'x'=4,'z'=12] {'yl'}, dimensions={0}, use_global_device_ids=true | all-gather | bytes 442368 | tf_op jit(solution)/shard_map/all_gather | solution.py:156
  41.7 3.4 %collective-permute-start.2 = (bf16[144,1024]{1,0:T(8,128)(2,1)S(1)}, bf16[144,1024]{1,0:T(8,128)(2,1)S(1)}, u32[]{:S(2)}, u32[]{:S(2)}) collective-permute-start(bf16[144,1024]{1,0:T(8,128)(2,1)S(1)} %all_gather.3.refs_0_), channel_id=1, source_target_pairs={{0,12},{12,24},{24,36},{36,0},{1,13},{13,25},{25,37},{37,1},{2,14}... | collective-permute-start | bytes 884744 | tf_op jit(solution)/shard_map/ppermute | solution.py:160
  45.1 3.0 %collective-permute-start.1 = (bf16[144,1024]{1,0:T(8,128)(2,1)S(1)}, bf16[144,1024]{1,0:T(8,128)(2,1)S(1)}, u32[]{:S(2)}, u32[]{:S(2)}) collective-permute-start(bf16[144,1024]{1,0:T(8,128)(2,1)S(1)} %all_gather.3.refs_0_), channel_id=1, source_target_pairs={{0,24},{12,36},{24,0},{36,12},{1,25},{13,37},{25,1},{37,13},{2,26}... | collective-permute-start | bytes 884744 | tf_op jit(solution)/shard_map/ppermute | solution.py:160
  48.1 4.1 %collective-permute-start = (bf16[144,1024]{1,0:T(8,128)(2,1)S(1)}, bf16[144,1024]{1,0:T(8,128)(2,1)S(1)}, u32[]{:S(2)}, u32[]{:S(2)}) collective-permute-start(bf16[144,1024]{1,0:T(8,128)(2,1)S(1)} %all_gather.3.refs_0_), channel_id=1, source_target_pairs={{0,36},{12,0},{24,12},{36,24},{1,37},{13,1},{25,13},{37,25},{2,38}... | collective-permute-start | bytes 884744 | tf_op jit(solution)/shard_map/ppermute | solution.py:160
  52.2 0.1 pad_add_fusion.place_ref
  52.2 0.3 collective-permute-done.2.refs_3_
  52.5 5.4 %collective-permute-done.1.refs_2_ = bf16[144,1024]{1,0:T(8,128)(2,1)S(1)} collective-permute-done((bf16[144,1024]{1,0:T(8,128)(2,1)S(1)}, bf16[144,1024]{1,0:T(8,128)(2,1)S(1)}, u32[]{:S(2)}, u32[]{:S(2)}) %collective-permute-start.1) | collective-permute-done | bytes 294944 | tf_op jit(solution)/shard_map/ppermute | solution.py:160
  57.9 3.0 %collective-permute-done.refs_1_ = bf16[144,1024]{1,0:T(8,128)(2,1)S(1)} collective-permute-done((bf16[144,1024]{1,0:T(8,128)(2,1)S(1)}, bf16[144,1024]{1,0:T(8,128)(2,1)S(1)}, u32[]{:S(2)}, u32[]{:S(2)}) %collective-permute-start) | collective-permute-done | bytes 294944 | tf_op jit(solution)/shard_map/ppermute | solution.py:160
  60.9 0.0 all-to-all-done.1
  60.9 0.0 copy-done
  60.9 5.6 %grads.1 = (bf16[4,384,128]{2,1,0:T(8,128)(2,1)S(1)}, f32[4,384,128]{2,1,0:T(8,128)S(1)}) custom-call(s32[2]{0:T(128)S(1)} %pad_add_fusion.place_ref, bf16[144,1024]{1,0:T(8,128)(2,1)S(1)} %all_gather.3.refs_0_, bf16[144,1024]{1,0:T(8,128)(2,1)S(1)} %collective-permute-done.refs_1_, bf16[144,1024]{1,0:T(8,128)(2,1)S(1)} %collective-permute-done.1.refs_2_, ...), custom_call_target="tpu_custom_call" | custom-call | tf_op jit(solution)/shard_map/grads/pallas_call | solution.py:124
  66.5 1.9 %collective-permute-start.3 = (bf16[4,384,128]{2,1,0:T(8,128)(2,1)S(1)}, bf16[4,384,128]{2,1,0:T(8,128)(2,1)S(1)}, u32[]{:S(2)}, u32[]{:S(2)}) collective-permute-start(bf16[4,384,128]{2,1,0:T(8,128)(2,1)S(1)} %get-tuple-element.8), channel_id=1, source_target_pairs={{0,96},{96,0},{1,97},{97,1},{2,98},{98,2},{3,99},{99,3},{4,100},{1... | collective-permute-start | bytes 1179656 | tf_op jit(solution)/shard_map/ppermute | solution.py:165
  68.5 1.7 %collective-permute-done.3 = bf16[4,384,128]{2,1,0:T(8,128)(2,1)S(1)} collective-permute-done((bf16[4,384,128]{2,1,0:T(8,128)(2,1)S(1)}, bf16[4,384,128]{2,1,0:T(8,128)(2,1)S(1)}, u32[]{:S(2)}, u32[]{:S(2)}) %collective-permute-start.3) | collective-permute-done | bytes 393248 | tf_op jit(solution)/shard_map/ppermute | solution.py:165
  70.2 0.1 add_convert_fusion
  70.2 38.6 %all_to_all.15 = bf16[48,32,128]{2,1,0:T(8,128)(2,1)S(1)} all-to-all(bf16[48,32,128]{2,1,0:T(8,128)(2,1)S(1)} %bitcast.7), channel_id=1, replica_groups=mesh['yh'=4,'core'=2,'yl'=2,'x'=4,'z'=12] {'yh','z'}, dimensions={0} | all-to-all | bytes 786432 | tf_op jit(solution)/shard_map/all_to_all | solution.py:168
  108.8 0.7 convert_reduce_fusion
Async XLA Ops:
  0.0 60.9 %copy-start = (bf16[3,1024,128]{2,1,0:T(8,128)(2,1)S(1)}, bf16[3,1024,128]{2,1,0:T(8,128)(2,1)}, u32[]{:S(2)}) copy-start(bf16[3,1024,128]{2,1,0:T(8,128)(2,1)} %refs_4_.1) | copy-start | bytes 2359300
  0.0 28.1 %all-to-all-start = ((bf16[12,48,128]{2,1,0:T(8,128)(2,1)}), bf16[12,48,128]{2,1,0:T(8,128)(2,1)S(1)}, u32[]{:S(2)}, u32[]{:S(2)}) async-start(bf16[12,48,128]{2,1,0:T(8,128)(2,1)} %bitcast.8), calls=%async_computation | async-start | bytes 294912 | tf_op jit(solution)/shard_map/all_to_all | solution.py:148
  29.6 3.7 %copy-start.1 = (bf16[1024]{0:T(1024)(128)(2,1)S(1)}, bf16[1024]{0:T(1024)(128)(2,1)}, u32[]{:S(2)}) copy-start(bf16[1024]{0:T(1024)(128)(2,1)} %param.12) | copy-start | bytes 6148
  29.6 31.3 %all-to-all-start.1 = ((bf16[12,48,128]{2,1,0:T(8,128)(2,1)}), bf16[12,48,128]{2,1,0:T(8,128)(2,1)S(1)}, u32[]{:S(2)}, u32[]{:S(2)}) async-start(bf16[12,48,128]{2,1,0:T(8,128)(2,1)} %route.1), calls=%async_computation.1 | async-start | bytes 294912 | tf_op jit(solution)/shard_map/all_to_all | solution.py:152
  41.7 10.8 %collective-permute-start.2 = (bf16[144,1024]{1,0:T(8,128)(2,1)S(1)}, bf16[144,1024]{1,0:T(8,128)(2,1)S(1)}, u32[]{:S(2)}, u32[]{:S(2)}) collective-permute-start(bf16[144,1024]{1,0:T(8,128)(2,1)S(1)} %all_gather.3.refs_0_), channel_id=1, source_target_pairs={{0,12},{12,24},{24,36},{36,0},{1,13},{13,25},{25,37},{37,1},{2,14}... | collective-permute-start | bytes 884744 | tf_op jit(solution)/shard_map/ppermute | solution.py:160
  45.1 12.9 %collective-permute-start.1 = (bf16[144,1024]{1,0:T(8,128)(2,1)S(1)}, bf16[144,1024]{1,0:T(8,128)(2,1)S(1)}, u32[]{:S(2)}, u32[]{:S(2)}) collective-permute-start(bf16[144,1024]{1,0:T(8,128)(2,1)S(1)} %all_gather.3.refs_0_), channel_id=1, source_target_pairs={{0,24},{12,36},{24,0},{36,12},{1,25},{13,37},{25,1},{37,13},{2,26}... | collective-permute-start | bytes 884744 | tf_op jit(solution)/shard_map/ppermute | solution.py:160
  48.1 12.8 %collective-permute-start = (bf16[144,1024]{1,0:T(8,128)(2,1)S(1)}, bf16[144,1024]{1,0:T(8,128)(2,1)S(1)}, u32[]{:S(2)}, u32[]{:S(2)}) collective-permute-start(bf16[144,1024]{1,0:T(8,128)(2,1)S(1)} %all_gather.3.refs_0_), channel_id=1, source_target_pairs={{0,36},{12,0},{24,12},{36,24},{1,37},{13,1},{25,13},{37,25},{2,38}... | collective-permute-start | bytes 884744 | tf_op jit(solution)/shard_map/ppermute | solution.py:160
  66.5 3.6 %collective-permute-start.3 = (bf16[4,384,128]{2,1,0:T(8,128)(2,1)S(1)}, bf16[4,384,128]{2,1,0:T(8,128)(2,1)S(1)}, u32[]{:S(2)}, u32[]{:S(2)}) collective-permute-start(bf16[4,384,128]{2,1,0:T(8,128)(2,1)S(1)} %get-tuple-element.8), channel_id=1, source_target_pairs={{0,96},{96,0},{1,97},{97,1},{2,98},{98,2},{3,99},{99,3},{4,100},{1... | collective-permute-start | bytes 1179656 | tf_op jit(solution)/shard_map/ppermute | solution.py:165
where the time goes:
time: 110 us
  blocking collectives  44.6 us (41%)
  starting transfers between devices  31.3 us (28%)
  waiting for transfers between devices  22.6 us (21%)
  Pallas kernels  8.84 us (8%)
    all_to_all x1, blocking collectives, step(): parts = lax.all_to_all(total, ('yh', 'z'), 0, 0, tiled=True)  38.6 us
    all_to_all x1, starting transfers between devices, step(): lax.all_to_all(dout[0, 0].reshape(seq_size, chunk, head_cols), 'z', 0, 0,...  15.3 us
    all_to_all x1, waiting for transfers between devices, step(): lax.all_to_all(dout[0, 0].reshape(seq_size, chunk, head_cols), 'z', 0, 0,...  12.2 us
    ppermute x3, starting transfers between devices, step(): normed.append(near(lax.ppermute(both, 'x', pairs)))  10.5 us
    ppermute x3, waiting for transfers between devices, step(): normed.append(near(lax.ppermute(both, 'x', pairs)))  8.69 us
    all_gather x1, blocking collectives, step(): both = lax.all_gather(local, 'yl', axis=0, tiled=True)  6.01 us
    pallas_call x1, Pallas kernels, weight_partials(): pl.pallas_call(grads_kernel, out_shape=(pltpu.VMEM(half, jnp.bfloat16), p...  5.6 us
    all_to_all x1, starting transfers between devices, step(): cotangent = lax.all_to_all(routed, 'z', 0, 0, tiled=True)  3.65 us
  transfers between devices with their start and end apart: 6, of which 5 were waited for; matrix products, arithmetic and copies ran while one was open for 1% of the time, Pallas kernels for 2%

commit v1 on v0

--- a/solution.py
+++ b/solution.py
@@ -1,3 +1,5 @@
+import functools
+
 import jax
 import jax.numpy as jnp
 from jax import lax
@@ -10,7 +12,7 @@
 GRP_OUTER = 4
 GRP_INNER = 2
 TP_OUTER = 2
-KERNEL_VMEM = 28 << 20
+KERNEL_VMEM = 24 << 20
 
 NN = (((1,), (0,)), ((), ()))
 NT = (((1,), (1,)), ((), ()))
@@ -30,7 +32,7 @@
     values = inputs_ref[...].astype(jnp.float32)
     centred = values - jnp.mean(values, axis=-1, keepdims=True)
     spread = jnp.mean(centred * centred, axis=-1, keepdims=True)
-    normed = centred * lax.rsqrt(spread + 1e-05) * gain_ref[...].astype(jnp.float32)
+    normed = centred * lax.rsqrt(spread + 1e-05) * gain_ref[...][None].astype(jnp.float32)
     out_ref[...] = normed.astype(jnp.bfloat16)
 
 
@@ -63,20 +65,54 @@
     )(count, ids, slots, pieces)
 
 
-def grads_kernel(place_ref, *refs):
-    *block_refs, weight_ref, cotangent_ref, theirs_ref, mine_ref, sums_ref = refs
+def head_mask(shape, head):
+    return lax.broadcasted_iota(jnp.int32, shape, 1) // HD == head
+
+
+def project_kernel(*refs):
+    *block_refs, weight_ref, projected_ref, normed_t_ref = refs
     low = jnp.bfloat16
-    both = block_refs[0].shape[0]
-    part = both // TP_OUTER
+    part = block_refs[0].shape[0] // TP_OUTER
     blocks = [ref[...] for ref in block_refs]
     normed = jnp.concatenate(
         [block[i * part : (i + 1) * part] for i in range(TP_OUTER) for block in blocks], 0
     )
-    tok_count, width = normed.shape
-    head_cols = cotangent_ref.shape[1]
-    queries = dot(normed, weight_ref[0]).astype(low)
-    key_rows = dot(normed, weight_ref[1]).astype(low)
-    value_rows = dot(normed, weight_ref[2]).astype(low)
+    for c in range(3):
+        projected_ref[c] = dot(normed, weight_ref[c]).astype(low)
+    normed_t_ref[...] = normed.T
+
+
+def project(normed, weight):
+    width, head_cols = weight.shape[1:]
+    tok_count = sum(block.shape[0] for block in normed)
+    return pl.pallas_call(
+        project_kernel,
+        out_shape=(
+            pltpu.VMEM((3, tok_count, head_cols), jnp.bfloat16),
+            pltpu.VMEM((width, tok_count), jnp.bfloat16),
+        ),
+        in_specs=[VMEM] * (len(normed) + 1),
+        out_specs=(VMEM, VMEM),
+        compiler_params=pltpu.CompilerParams(vmem_limit_bytes=KERNEL_VMEM),
+        name="project",
+    )(*normed, weight)
+
+
+def grads_kernel(
+    place_ref,
+    projected_ref,
+    normed_t_ref,
+    cotangent_ref,
+    theirs_ref,
+    mine_ref,
+    sums_ref,
+    *,
+    part,
+):
+    low = jnp.bfloat16
+    tok_count, head_cols = cotangent_ref.shape
+    width = normed_t_ref.shape[0]
+    queries, key_rows, value_rows = projected_ref[0], projected_ref[1], projected_ref[2]
     half = tok_count // TP_OUTER
     first = place_ref[1] * part
     turn = jnp.where(first == 0, 0, half - first)
@@ -84,14 +120,14 @@
     upstream = jnp.concatenate(
         [pltpu.roll(upstream[i * half : (i + 1) * half], turn, 0) for i in range(TP_OUTER)], 0
     ).astype(low)
-    head_of = lax.broadcasted_iota(jnp.int32, (tok_count, head_cols), 1) // HD
     zero = jnp.zeros((), low)
     score_scale = HD ** (-0.5)
     keys_t = key_rows.T
     grad_values, grad_keys, grad_queries = [], [], []
     for head in range(head_cols // HD):
-        q = jnp.where(head_of == head, queries, zero)
-        g = jnp.where(head_of == head, upstream, zero)
+        own = head_mask(queries.shape, head)
+        q = jnp.where(own, queries, zero)
+        g = jnp.where(own, upstream, zero)
         scores = dot(key_rows, q, NT) * score_scale
         weights = jnp.exp(scores - jnp.max(scores, axis=0, keepdims=True))
         attention = weights / jnp.sum(weights, axis=0, keepdims=True)
@@ -101,7 +137,7 @@
         grad_values.append(dot(attention.astype(low), g))
         grad_keys.append(dot(scaled, q))
         grad_queries.append(dot(keys_t[head * HD : (head + 1) * HD], scaled))
-    normed_t = normed.T
+    normed_t = normed_t_ref[...]
     joined = (
         jnp.concatenate(grad_queries, 0).astype(low).T,
         sum(grad_keys).astype(low),
@@ -118,21 +154,21 @@
         theirs_ref[outer] = sums_ref[pl.ds(other, rows), :].astype(low)
 
 
-def weight_partials(place, normed, weight, cotangent):
-    width, head_cols = weight.shape[1:]
+def weight_partials(place, projected, normed_t, cotangent, part):
+    width, head_cols = normed_t.shape[0], cotangent.shape[1]
     half = (GRP_OUTER, 3 * width // (GRP_OUTER * GRP_INNER), head_cols)
     return pl.pallas_call(
-        grads_kernel,
+        functools.partial(grads_kernel, part=part),
         out_shape=(
             pltpu.VMEM(half, jnp.bfloat16),
             pltpu.VMEM(half, jnp.float32),
         ),
-        in_specs=[SMEM, *[VMEM] * len(normed), VMEM, VMEM],
+        in_specs=[SMEM, VMEM, VMEM, VMEM],
         out_specs=(VMEM, VMEM),
         scratch_shapes=[pltpu.VMEM((3 * width, head_cols), jnp.float32)],
         compiler_params=pltpu.CompilerParams(vmem_limit_bytes=KERNEL_VMEM),
         name="grads",
-    )(place, *normed, weight, cotangent)
+    )(place, projected, normed_t, cotangent)
 
 
 def make_body(seq_size):
@@ -152,15 +188,18 @@
         cotangent = lax.all_to_all(routed, "z", 0, 0, tiled=True)
         cotangent = cotangent.reshape(tok_count, head_cols)
 
-        local = layer_norm(crops[0, 0], norm_gain[None])
+        local = layer_norm(crops[0, 0], norm_gain)
         both = lax.all_gather(local, "yl", axis=0, tiled=True)
         normed = [near(both)]
         for d in range(1, tp_inner):
             pairs = [(i, (i - d) % tp_inner) for i in range(tp_inner)]
             normed.append(near(lax.ppermute(both, "x", pairs)))
 
+        kept = project(normed, qkv_weight)
         place = jnp.stack([lax.axis_index("core"), lax.axis_index("x")])
-        theirs, mine = weight_partials(place, normed, near(qkv_weight), near(cotangent))
+        theirs, mine = weight_partials(
+            place, *[near(value) for value in kept], near(cotangent), tok_local
+        )
 
         received = lax.ppermute(theirs, "core", [(0, 1), (1, 0)])
         total = (mine + received.astype(jnp.float32)).astype(jnp.bfloat16)

time: 110 us -> 112 us (1.018)
  local copies, waits for them, and re-layouts: 0.6 us -> 3.36 us
    unnamed x4 -> x10, local copies, waits for them, and re-layouts: 0.01 us -> 3.36 us
    pallas_call x1 -> x2, Pallas kernels: 5.6 us -> 5.77 us  [the longest x1 4.69 us: weight_partials(): pl.pallas_call(functools.partial(grads_kernel, part=part), out_shape=(plt...]
  transfers between devices with their start and end apart: 6 -> 6, of which waited for: 5 -> 5; matrix products, arithmetic and copies ran while one was open for 1% -> 0% of each run, Pallas kernels for 2% -> 3%
where the time goes in v1:
time: 112 us
  blocking collectives  44.9 us (40%)
  starting transfers between devices  31.2 us (28%)
  waiting for transfers between devices  21.9 us (20%)
  Pallas kernels  9.02 us (8%)
  local copies, waits for them, and re-layouts  3.36 us (3%)
    all_to_all x1, blocking collectives, step(): parts = lax.all_to_all(total, ('yh', 'z'), 0, 0, tiled=True)  38.9 us
    all_to_all x1, starting transfers between devices, step(): lax.all_to_all(dout[0, 0].reshape(seq_size, chunk, head_cols), 'z', 0, 0,...  15.3 us
    all_to_all x1, waiting for transfers between devices, step(): lax.all_to_all(dout[0, 0].reshape(seq_size, chunk, head_cols), 'z', 0, 0,...  12.2 us
    ppermute x3, starting transfers between devices, step(): normed.append(near(lax.ppermute(both, 'x', pairs)))  10.5 us
    ppermute x3, waiting for transfers between devices, step(): normed.append(near(lax.ppermute(both, 'x', pairs)))  7.98 us
    all_gather x1, blocking collectives, step(): both = lax.all_gather(local, 'yl', axis=0, tiled=True)  6.01 us
    pallas_call x1, Pallas kernels, weight_partials(): pl.pallas_call(functools.partial(grads_kernel, part=part), out_shape=(plt...  4.69 us
    all_to_all x1, starting transfers between devices, step(): cotangent = lax.all_to_all(routed, 'z', 0, 0, tiled=True)  3.52 us
  transfers between devices with their start and end apart: 6, of which 5 were waited for; matrix products, arithmetic and copies ran while one was open for 0% of the time, Pallas kernels for 3%

profile of v1, /device:TPU:2, one launch (start us, length us, event | category | flops | bytes accessed | tf_op | source)
XLA Modules:
  0.0 111.9 jit_solution(18029416266328838122)
XLA Ops:
  0.0 0.0 copy-start
  0.0 15.3 %all-to-all-start = ((bf16[12,48,128]{2,1,0:T(8,128)(2,1)}), bf16[12,48,128]{2,1,0:T(8,128)(2,1)S(1)}, u32[]{:S(2)}, u32[]{:S(2)}) async-start(bf16[12,48,128]{2,1,0:T(8,128)(2,1)} %bitcast.8), calls=%async_computation | async-start | bytes 294912 | tf_op jit(solution)/shard_map/all_to_all | solution.py:184
  15.9 12.2 %all-to-all-done.pieces_ref = bf16[12,48,128]{2,1,0:T(8,128)(2,1)S(1)} async-done(((bf16[12,48,128]{2,1,0:T(8,128)(2,1)}), bf16[12,48,128]{2,1,0:T(8,128)(2,1)S(1)}, u32[]{:S(2)}, u32[]{:S(2)}) %all-to-all-start) | async-done | bytes 147488 | tf_op jit(solution)/shard_map/all_to_all | solution.py:184
  28.1 1.5 %route.1 = bf16[12,48,128]{2,1,0:T(8,128)(2,1)} custom-call(s32[1]{0:T(128)S(6)} %copy.8.count_ref, s32[1,12]{1,0:T(1,128)} %ids_ref.1, s32[1,12]{1,0:T(1,128)} %slot_ref.1, bf16[12,48,128]{2,1,0:T(8,128)(2,1)S(1)} %all-to-all-done.pieces_ref), custom_call_target="tpu_custom_call" | custom-call | tf_op jit(solution)/shard_map/route/pallas_call | solution.py:59
  29.6 3.5 %all-to-all-start.1 = ((bf16[12,48,128]{2,1,0:T(8,128)(2,1)}), bf16[12,48,128]{2,1,0:T(8,128)(2,1)S(1)}, u32[]{:S(2)}, u32[]{:S(2)}) async-start(bf16[12,48,128]{2,1,0:T(8,128)(2,1)} %route.1), calls=%async_computation.1 | async-start | bytes 294912 | tf_op jit(solution)/shard_map/all_to_all | solution.py:188
  33.1 1.8 %norm.1 = bf16[72,1024]{1,0:T(8,128)(2,1)} custom-call(bf16[72,1024]{1,0:T(8,128)(2,1)} %bitcast.9, bf16[1024]{0:T(1024)(128)(2,1)} %gain_ref.1), custom_call_target="tpu_custom_call" | custom-call | tf_op jit(solution)/shard_map/norm/pallas_call | solution.py:40
  34.9 6.0 %all_gather.3.refs_0_ = bf16[144,1024]{1,0:T(8,128)(2,1)S(1)} all-gather(bf16[72,1024]{1,0:T(8,128)(2,1)} %norm.1), channel_id=1, replica_groups=mesh['yh'=4,'core'=2,'yl'=2,'x'=4,'z'=12] {'yl'}, dimensions={0}, use_global_device_ids=true | all-gather | bytes 442368 | tf_op jit(solution)/shard_map/all_gather | solution.py:192
  40.9 3.4 %collective-permute-start.2 = (bf16[144,1024]{1,0:T(8,128)(2,1)S(1)}, bf16[144,1024]{1,0:T(8,128)(2,1)S(1)}, u32[]{:S(2)}, u32[]{:S(2)}) collective-permute-start(bf16[144,1024]{1,0:T(8,128)(2,1)S(1)} %all_gather.3.refs_0_), channel_id=1, source_target_pairs={{0,12},{12,24},{24,36},{36,0},{1,13},{13,25},{25,37},{37,1},{2,14}... | collective-permute-start | bytes 884744 | tf_op jit(solution)/shard_map/ppermute | solution.py:196
  44.3 3.0 %collective-permute-start.1 = (bf16[144,1024]{1,0:T(8,128)(2,1)S(1)}, bf16[144,1024]{1,0:T(8,128)(2,1)S(1)}, u32[]{:S(2)}, u32[]{:S(2)}) collective-permute-start(bf16[144,1024]{1,0:T(8,128)(2,1)S(1)} %all_gather.3.refs_0_), channel_id=1, source_target_pairs={{0,24},{12,36},{24,0},{36,12},{1,25},{13,37},{25,1},{37,13},{2,26}... | collective-permute-start | bytes 884744 | tf_op jit(solution)/shard_map/ppermute | solution.py:196
  47.4 4.1 %collective-permute-start = (bf16[144,1024]{1,0:T(8,128)(2,1)S(1)}, bf16[144,1024]{1,0:T(8,128)(2,1)S(1)}, u32[]{:S(2)}, u32[]{:S(2)}) collective-permute-start(bf16[144,1024]{1,0:T(8,128)(2,1)S(1)} %all_gather.3.refs_0_), channel_id=1, source_target_pairs={{0,36},{12,0},{24,12},{36,24},{1,37},{13,1},{25,13},{37,25},{2,38}... | collective-permute-start | bytes 884744 | tf_op jit(solution)/shard_map/ppermute | solution.py:196
  51.4 0.1 pad_add_fusion.place_ref
  51.5 0.3 collective-permute-done.2.refs_3_
  51.8 5.4 %collective-permute-done.1.refs_2_ = bf16[144,1024]{1,0:T(8,128)(2,1)S(1)} collective-permute-done((bf16[144,1024]{1,0:T(8,128)(2,1)S(1)}, bf16[144,1024]{1,0:T(8,128)(2,1)S(1)}, u32[]{:S(2)}, u32[]{:S(2)}) %collective-permute-start.1) | collective-permute-done | bytes 294944 | tf_op jit(solution)/shard_map/ppermute | solution.py:196
  57.2 0.0 copy-start.1
  57.2 0.7 copy-done.1
  57.9 2.3 %collective-permute-done.refs_1_ = bf16[144,1024]{1,0:T(8,128)(2,1)S(1)} collective-permute-done((bf16[144,1024]{1,0:T(8,128)(2,1)S(1)}, bf16[144,1024]{1,0:T(8,128)(2,1)S(1)}, u32[]{:S(2)}, u32[]{:S(2)}) %collective-permute-start) | collective-permute-done | bytes 294944 | tf_op jit(solution)/shard_map/ppermute | solution.py:196
  60.2 0.0 copy-start.3
  60.2 0.7 copy-done.3
  60.9 0.0 copy-done
  60.9 0.0 copy-start.2
  60.9 1.0 copy-done.2
  61.9 0.0 copy-start.4
  61.9 1.0 copy-done.4
  62.8 1.1 project.1
  63.9 0.0 all-to-all-done.1
  63.9 4.7 %grads.1 = (bf16[4,384,128]{2,1,0:T(8,128)(2,1)S(1)}, f32[4,384,128]{2,1,0:T(8,128)S(1)}) custom-call(s32[2]{0:T(128)S(1)} %pad_add_fusion.place_ref, bf16[3,576,128]{2,1,0:T(8,128)(2,1)S(1)} %get-tuple-element.9.projected_ref, bf16[1024,576]{1,0:T(8,128)(2,1)S(1)} %get-tuple-element.10.normed_t_ref, bf16[576,128]{1,0:T(8,128)(2,1)S(1)} %bitcast.6), custom_call_target="tpu_custom_call" | custom-call | tf_op jit(solution)/shard_map/grads/pallas_call | solution.py:160
  68.6 1.9 %collective-permute-start.3 = (bf16[4,384,128]{2,1,0:T(8,128)(2,1)S(1)}, bf16[4,384,128]{2,1,0:T(8,128)(2,1)S(1)}, u32[]{:S(2)}, u32[]{:S(2)}) collective-permute-start(bf16[4,384,128]{2,1,0:T(8,128)(2,1)S(1)} %get-tuple-element.12), channel_id=1, source_target_pairs={{0,96},{96,0},{1,97},{97,1},{2,98},{98,2},{3,99},{99,3},{4,100},{1... | collective-permute-start | bytes 1179656 | tf_op jit(solution)/shard_map/ppermute | solution.py:204
  70.6 1.7 %collective-permute-done.3 = bf16[4,384,128]{2,1,0:T(8,128)(2,1)S(1)} collective-permute-done((bf16[4,384,128]{2,1,0:T(8,128)(2,1)S(1)}, bf16[4,384,128]{2,1,0:T(8,128)(2,1)S(1)}, u32[]{:S(2)}, u32[]{:S(2)}) %collective-permute-start.3) | collective-permute-done | bytes 393248 | tf_op jit(solution)/shard_map/ppermute | solution.py:204
  72.3 0.1 add_convert_fusion
  72.3 38.9 %all_to_all.15 = bf16[48,32,128]{2,1,0:T(8,128)(2,1)S(1)} all-to-all(bf16[48,32,128]{2,1,0:T(8,128)(2,1)S(1)} %bitcast.7), channel_id=1, replica_groups=mesh['yh'=4,'core'=2,'yl'=2,'x'=4,'z'=12] {'yh','z'}, dimensions={0} | all-to-all | bytes 786432 | tf_op jit(solution)/shard_map/all_to_all | solution.py:207
  111.2 0.7 convert_reduce_fusion
Async XLA Ops:
  0.0 60.9 %copy-start = (bf16[3,1024,128]{2,1,0:T(8,128)(2,1)S(1)}, bf16[3,1024,128]{2,1,0:T(8,128)(2,1)}, u32[]{:S(2)}) copy-start(bf16[3,1024,128]{2,1,0:T(8,128)(2,1)} %refs_4_.1) | copy-start | bytes 2359300
  0.0 28.1 %all-to-all-start = ((bf16[12,48,128]{2,1,0:T(8,128)(2,1)}), bf16[12,48,128]{2,1,0:T(8,128)(2,1)S(1)}, u32[]{:S(2)}, u32[]{:S(2)}) async-start(bf16[12,48,128]{2,1,0:T(8,128)(2,1)} %bitcast.8), calls=%async_computation | async-start | bytes 294912 | tf_op jit(solution)/shard_map/all_to_all | solution.py:184
  29.6 34.3 %all-to-all-start.1 = ((bf16[12,48,128]{2,1,0:T(8,128)(2,1)}), bf16[12,48,128]{2,1,0:T(8,128)(2,1)S(1)}, u32[]{:S(2)}, u32[]{:S(2)}) async-start(bf16[12,48,128]{2,1,0:T(8,128)(2,1)} %route.1), calls=%async_computation.1 | async-start | bytes 294912 | tf_op jit(solution)/shard_map/all_to_all | solution.py:188
  40.9 10.8 %collective-permute-start.2 = (bf16[144,1024]{1,0:T(8,128)(2,1)S(1)}, bf16[144,1024]{1,0:T(8,128)(2,1)S(1)}, u32[]{:S(2)}, u32[]{:S(2)}) collective-permute-start(bf16[144,1024]{1,0:T(8,128)(2,1)S(1)} %all_gather.3.refs_0_), channel_id=1, source_target_pairs={{0,12},{12,24},{24,36},{36,0},{1,13},{13,25},{25,37},{37,1},{2,14}... | collective-permute-start | bytes 884744 | tf_op jit(solution)/shard_map/ppermute | solution.py:196
  44.3 12.9 %collective-permute-start.1 = (bf16[144,1024]{1,0:T(8,128)(2,1)S(1)}, bf16[144,1024]{1,0:T(8,128)(2,1)S(1)}, u32[]{:S(2)}, u32[]{:S(2)}) collective-permute-start(bf16[144,1024]{1,0:T(8,128)(2,1)S(1)} %all_gather.3.refs_0_), channel_id=1, source_target_pairs={{0,24},{12,36},{24,0},{36,12},{1,25},{13,37},{25,1},{37,13},{2,26}... | collective-permute-start | bytes 884744 | tf_op jit(solution)/shard_map/ppermute | solution.py:196
  47.4 12.8 %collective-permute-start = (bf16[144,1024]{1,0:T(8,128)(2,1)S(1)}, bf16[144,1024]{1,0:T(8,128)(2,1)S(1)}, u32[]{:S(2)}, u32[]{:S(2)}) collective-permute-start(bf16[144,1024]{1,0:T(8,128)(2,1)S(1)} %all_gather.3.refs_0_), channel_id=1, source_target_pairs={{0,36},{12,0},{24,12},{36,24},{1,37},{13,1},{25,13},{37,25},{2,38}... | collective-permute-start | bytes 884744 | tf_op jit(solution)/shard_map/ppermute | solution.py:196
  57.2 0.7 copy-start.1
  60.2 0.7 copy-start.3
  60.9 1.0 copy-start.2
  61.9 1.0 copy-start.4
  68.6 3.6 %collective-permute-start.3 = (bf16[4,384,128]{2,1,0:T(8,128)(2,1)S(1)}, bf16[4,384,128]{2,1,0:T(8,128)(2,1)S(1)}, u32[]{:S(2)}, u32[]{:S(2)}) collective-permute-start(bf16[4,384,128]{2,1,0:T(8,128)(2,1)S(1)} %get-tuple-element.12), channel_id=1, source_target_pairs={{0,96},{96,0},{1,97},{97,1},{2,98},{98,2},{3,99},{99,3},{4,100},{1... | collective-permute-start | bytes 1179656 | tf_op jit(solution)/shard_map/ppermute | solution.py:204

commit v2 on v1

--- a/solution.py
+++ b/solution.py
@@ -121,19 +121,19 @@
         [pltpu.roll(upstream[i * half : (i + 1) * half], turn, 0) for i in range(TP_OUTER)], 0
     ).astype(low)
     zero = jnp.zeros((), low)
-    score_scale = HD ** (-0.5)
+    score_scale = jnp.asarray(HD ** (-0.5), low)
     keys_t = key_rows.T
     grad_values, grad_keys, grad_queries = [], [], []
     for head in range(head_cols // HD):
         own = head_mask(queries.shape, head)
         q = jnp.where(own, queries, zero)
         g = jnp.where(own, upstream, zero)
-        scores = dot(key_rows, q, NT) * score_scale
+        scores = dot(key_rows, q * score_scale, NT)
         weights = jnp.exp(scores - jnp.max(scores, axis=0, keepdims=True))
-        attention = weights / jnp.sum(weights, axis=0, keepdims=True)
-        grad_attention = dot(value_rows, g, NT)
+        attention = weights * (1.0 / jnp.sum(weights, axis=0, keepdims=True))
+        grad_attention = dot(value_rows, g * score_scale, NT)
         mean = jnp.sum(attention * grad_attention, axis=0, keepdims=True)
-        scaled = (attention * (grad_attention - mean) * score_scale).astype(low)
+        scaled = (attention * (grad_attention - mean)).astype(low)
         grad_values.append(dot(attention.astype(low), g))
         grad_keys.append(dot(scaled, q))
         grad_queries.append(dot(keys_t[head * HD : (head + 1) * HD], scaled))

time: 112 us -> 112 us (level)
  no operation moved by 1% of the time
where the time goes in v2:
time: 112 us
  blocking collectives  44.9 us (40%)
  starting transfers between devices  31.2 us (28%)
  waiting for transfers between devices  21.9 us (20%)
  Pallas kernels  8.89 us (8%)
  local copies, waits for them, and re-layouts  3.36 us (3%)
    all_to_all x1, blocking collectives, step(): parts = lax.all_to_all(total, ('yh', 'z'), 0, 0, tiled=True)  38.9 us
    all_to_all x1, starting transfers between devices, step(): lax.all_to_all(dout[0, 0].reshape(seq_size, chunk, head_cols), 'z', 0, 0,...  15.3 us
    all_to_all x1, waiting for transfers between devices, step(): lax.all_to_all(dout[0, 0].reshape(seq_size, chunk, head_cols), 'z', 0, 0,...  12.2 us
    ppermute x3, starting transfers between devices, step(): normed.append(near(lax.ppermute(both, 'x', pairs)))  10.5 us
    ppermute x3, waiting for transfers between devices, step(): normed.append(near(lax.ppermute(both, 'x', pairs)))  7.98 us
    all_gather x1, blocking collectives, step(): both = lax.all_gather(local, 'yl', axis=0, tiled=True)  6.01 us
    pallas_call x1, Pallas kernels, weight_partials(): pl.pallas_call(functools.partial(grads_kernel, part=part), out_shape=(plt...  4.56 us
    all_to_all x1, starting transfers between devices, step(): cotangent = lax.all_to_all(routed, 'z', 0, 0, tiled=True)  3.52 us
  transfers between devices with their start and end apart: 6, of which 5 were waited for; matrix products, arithmetic and copies ran while one was open for 0% of the time, Pallas kernels for 3%

profile of v2, /device:TPU:2, one launch (start us, length us, event | category | flops | bytes accessed | tf_op | source)
XLA Modules:
  0.0 111.8 jit_solution(2962683791971936512)
XLA Ops:
  0.0 0.0 copy-start
  0.0 15.3 %all-to-all-start = ((bf16[12,48,128]{2,1,0:T(8,128)(2,1)}), bf16[12,48,128]{2,1,0:T(8,128)(2,1)S(1)}, u32[]{:S(2)}, u32[]{:S(2)}) async-start(bf16[12,48,128]{2,1,0:T(8,128)(2,1)} %bitcast.8), calls=%async_computation | async-start | bytes 294912 | tf_op jit(solution)/shard_map/all_to_all | solution.py:184
  15.9 12.2 %all-to-all-done.pieces_ref = bf16[12,48,128]{2,1,0:T(8,128)(2,1)S(1)} async-done(((bf16[12,48,128]{2,1,0:T(8,128)(2,1)}), bf16[12,48,128]{2,1,0:T(8,128)(2,1)S(1)}, u32[]{:S(2)}, u32[]{:S(2)}) %all-to-all-start) | async-done | bytes 147488 | tf_op jit(solution)/shard_map/all_to_all | solution.py:184
  28.1 1.5 %route.1 = bf16[12,48,128]{2,1,0:T(8,128)(2,1)} custom-call(s32[1]{0:T(128)S(6)} %copy.8.count_ref, s32[1,12]{1,0:T(1,128)} %ids_ref.1, s32[1,12]{1,0:T(1,128)} %slot_ref.1, bf16[12,48,128]{2,1,0:T(8,128)(2,1)S(1)} %all-to-all-done.pieces_ref), custom_call_target="tpu_custom_call" | custom-call | tf_op jit(solution)/shard_map/route/pallas_call | solution.py:59
  29.6 3.5 %all-to-all-start.1 = ((bf16[12,48,128]{2,1,0:T(8,128)(2,1)}), bf16[12,48,128]{2,1,0:T(8,128)(2,1)S(1)}, u32[]{:S(2)}, u32[]{:S(2)}) async-start(bf16[12,48,128]{2,1,0:T(8,128)(2,1)} %route.1), calls=%async_computation.1 | async-start | bytes 294912 | tf_op jit(solution)/shard_map/all_to_all | solution.py:188
  33.1 1.8 %norm.1 = bf16[72,1024]{1,0:T(8,128)(2,1)} custom-call(bf16[72,1024]{1,0:T(8,128)(2,1)} %bitcast.9, bf16[1024]{0:T(1024)(128)(2,1)} %gain_ref.1), custom_call_target="tpu_custom_call" | custom-call | tf_op jit(solution)/shard_map/norm/pallas_call | solution.py:40
  34.9 6.0 %all_gather.3.refs_0_ = bf16[144,1024]{1,0:T(8,128)(2,1)S(1)} all-gather(bf16[72,1024]{1,0:T(8,128)(2,1)} %norm.1), channel_id=1, replica_groups=mesh['yh'=4,'core'=2,'yl'=2,'x'=4,'z'=12] {'yl'}, dimensions={0}, use_global_device_ids=true | all-gather | bytes 442368 | tf_op jit(solution)/shard_map/all_gather | solution.py:192
  40.9 3.4 %collective-permute-start.2 = (bf16[144,1024]{1,0:T(8,128)(2,1)S(1)}, bf16[144,1024]{1,0:T(8,128)(2,1)S(1)}, u32[]{:S(2)}, u32[]{:S(2)}) collective-permute-start(bf16[144,1024]{1,0:T(8,128)(2,1)S(1)} %all_gather.3.refs_0_), channel_id=1, source_target_pairs={{0,12},{12,24},{24,36},{36,0},{1,13},{13,25},{25,37},{37,1},{2,14}... | collective-permute-start | bytes 884744 | tf_op jit(solution)/shard_map/ppermute | solution.py:196
  44.3 3.0 %collective-permute-start.1 = (bf16[144,1024]{1,0:T(8,128)(2,1)S(1)}, bf16[144,1024]{1,0:T(8,128)(2,1)S(1)}, u32[]{:S(2)}, u32[]{:S(2)}) collective-permute-start(bf16[144,1024]{1,0:T(8,128)(2,1)S(1)} %all_gather.3.refs_0_), channel_id=1, source_target_pairs={{0,24},{12,36},{24,0},{36,12},{1,25},{13,37},{25,1},{37,13},{2,26}... | collective-permute-start | bytes 884744 | tf_op jit(solution)/shard_map/ppermute | solution.py:196
  47.4 4.1 %collective-permute-start = (bf16[144,1024]{1,0:T(8,128)(2,1)S(1)}, bf16[144,1024]{1,0:T(8,128)(2,1)S(1)}, u32[]{:S(2)}, u32[]{:S(2)}) collective-permute-start(bf16[144,1024]{1,0:T(8,128)(2,1)S(1)} %all_gather.3.refs_0_), channel_id=1, source_target_pairs={{0,36},{12,0},{24,12},{36,24},{1,37},{13,1},{25,13},{37,25},{2,38}... | collective-permute-start | bytes 884744 | tf_op jit(solution)/shard_map/ppermute | solution.py:196
  51.4 0.1 pad_add_fusion.place_ref
  51.5 0.3 collective-permute-done.2.refs_3_
  51.8 5.4 %collective-permute-done.1.refs_2_ = bf16[144,1024]{1,0:T(8,128)(2,1)S(1)} collective-permute-done((bf16[144,1024]{1,0:T(8,128)(2,1)S(1)}, bf16[144,1024]{1,0:T(8,128)(2,1)S(1)}, u32[]{:S(2)}, u32[]{:S(2)}) %collective-permute-start.1) | collective-permute-done | bytes 294944 | tf_op jit(solution)/shard_map/ppermute | solution.py:196
  57.2 0.0 copy-start.1
  57.2 0.7 copy-done.1
  57.9 2.3 %collective-permute-done.refs_1_ = bf16[144,1024]{1,0:T(8,128)(2,1)S(1)} collective-permute-done((bf16[144,1024]{1,0:T(8,128)(2,1)S(1)}, bf16[144,1024]{1,0:T(8,128)(2,1)S(1)}, u32[]{:S(2)}, u32[]{:S(2)}) %collective-permute-start) | collective-permute-done | bytes 294944 | tf_op jit(solution)/shard_map/ppermute | solution.py:196
  60.2 0.0 copy-start.3
  60.2 0.7 copy-done.3
  60.9 0.0 copy-done
  60.9 0.0 copy-start.2
  60.9 1.0 copy-done.2
  61.9 0.0 copy-start.4
  61.9 1.0 copy-done.4
  62.8 1.1 project.1
  63.9 0.0 all-to-all-done.1
  63.9 4.6 %grads.1 = (bf16[4,384,128]{2,1,0:T(8,128)(2,1)S(1)}, f32[4,384,128]{2,1,0:T(8,128)S(1)}) custom-call(s32[2]{0:T(128)S(1)} %pad_add_fusion.place_ref, bf16[3,576,128]{2,1,0:T(8,128)(2,1)S(1)} %get-tuple-element.9.projected_ref, bf16[1024,576]{1,0:T(8,128)(2,1)S(1)} %get-tuple-element.10.normed_t_ref, bf16[576,128]{1,0:T(8,128)(2,1)S(1)} %bitcast.6), custom_call_target="tpu_custom_call" | custom-call | tf_op jit(solution)/shard_map/grads/pallas_call | solution.py:160
  68.5 1.9 %collective-permute-start.3 = (bf16[4,384,128]{2,1,0:T(8,128)(2,1)S(1)}, bf16[4,384,128]{2,1,0:T(8,128)(2,1)S(1)}, u32[]{:S(2)}, u32[]{:S(2)}) collective-permute-start(bf16[4,384,128]{2,1,0:T(8,128)(2,1)S(1)} %get-tuple-element.12), channel_id=1, source_target_pairs={{0,96},{96,0},{1,97},{97,1},{2,98},{98,2},{3,99},{99,3},{4,100},{1... | collective-permute-start | bytes 1179656 | tf_op jit(solution)/shard_map/ppermute | solution.py:204
  70.4 1.7 %collective-permute-done.3 = bf16[4,384,128]{2,1,0:T(8,128)(2,1)S(1)} collective-permute-done((bf16[4,384,128]{2,1,0:T(8,128)(2,1)S(1)}, bf16[4,384,128]{2,1,0:T(8,128)(2,1)S(1)}, u32[]{:S(2)}, u32[]{:S(2)}) %collective-permute-start.3) | collective-permute-done | bytes 393248 | tf_op jit(solution)/shard_map/ppermute | solution.py:204
  72.1 0.1 add_convert_fusion
  72.2 38.9 %all_to_all.15 = bf16[48,32,128]{2,1,0:T(8,128)(2,1)S(1)} all-to-all(bf16[48,32,128]{2,1,0:T(8,128)(2,1)S(1)} %bitcast.7), channel_id=1, replica_groups=mesh['yh'=4,'core'=2,'yl'=2,'x'=4,'z'=12] {'yh','z'}, dimensions={0} | all-to-all | bytes 786432 | tf_op jit(solution)/shard_map/all_to_all | solution.py:207
  111.1 0.7 convert_reduce_fusion
Async XLA Ops:
  0.0 60.9 %copy-start = (bf16[3,1024,128]{2,1,0:T(8,128)(2,1)S(1)}, bf16[3,1024,128]{2,1,0:T(8,128)(2,1)}, u32[]{:S(2)}) copy-start(bf16[3,1024,128]{2,1,0:T(8,128)(2,1)} %refs_4_.1) | copy-start | bytes 2359300
  0.0 28.1 %all-to-all-start = ((bf16[12,48,128]{2,1,0:T(8,128)(2,1)}), bf16[12,48,128]{2,1,0:T(8,128)(2,1)S(1)}, u32[]{:S(2)}, u32[]{:S(2)}) async-start(bf16[12,48,128]{2,1,0:T(8,128)(2,1)} %bitcast.8), calls=%async_computation | async-start | bytes 294912 | tf_op jit(solution)/shard_map/all_to_all | solution.py:184
  29.6 34.3 %all-to-all-start.1 = ((bf16[12,48,128]{2,1,0:T(8,128)(2,1)}), bf16[12,48,128]{2,1,0:T(8,128)(2,1)S(1)}, u32[]{:S(2)}, u32[]{:S(2)}) async-start(bf16[12,48,128]{2,1,0:T(8,128)(2,1)} %route.1), calls=%async_computation.1 | async-start | bytes 294912 | tf_op jit(solution)/shard_map/all_to_all | solution.py:188
  40.9 10.8 %collective-permute-start.2 = (bf16[144,1024]{1,0:T(8,128)(2,1)S(1)}, bf16[144,1024]{1,0:T(8,128)(2,1)S(1)}, u32[]{:S(2)}, u32[]{:S(2)}) collective-permute-start(bf16[144,1024]{1,0:T(8,128)(2,1)S(1)} %all_gather.3.refs_0_), channel_id=1, source_target_pairs={{0,12},{12,24},{24,36},{36,0},{1,13},{13,25},{25,37},{37,1},{2,14}... | collective-permute-start | bytes 884744 | tf_op jit(solution)/shard_map/ppermute | solution.py:196
  44.3 12.9 %collective-permute-start.1 = (bf16[144,1024]{1,0:T(8,128)(2,1)S(1)}, bf16[144,1024]{1,0:T(8,128)(2,1)S(1)}, u32[]{:S(2)}, u32[]{:S(2)}) collective-permute-start(bf16[144,1024]{1,0:T(8,128)(2,1)S(1)} %all_gather.3.refs_0_), channel_id=1, source_target_pairs={{0,24},{12,36},{24,0},{36,12},{1,25},{13,37},{25,1},{37,13},{2,26}... | collective-permute-start | bytes 884744 | tf_op jit(solution)/shard_map/ppermute | solution.py:196
  47.4 12.8 %collective-permute-start = (bf16[144,1024]{1,0:T(8,128)(2,1)S(1)}, bf16[144,1024]{1,0:T(8,128)(2,1)S(1)}, u32[]{:S(2)}, u32[]{:S(2)}) collective-permute-start(bf16[144,1024]{1,0:T(8,128)(2,1)S(1)} %all_gather.3.refs_0_), channel_id=1, source_target_pairs={{0,36},{12,0},{24,12},{36,24},{1,37},{13,1},{25,13},{37,25},{2,38}... | collective-permute-start | bytes 884744 | tf_op jit(solution)/shard_map/ppermute | solution.py:196
  57.2 0.7 copy-start.1
  60.2 0.7 copy-start.3
  60.9 1.0 copy-start.2
  61.9 1.0 copy-start.4
  68.5 3.6 %collective-permute-start.3 = (bf16[4,384,128]{2,1,0:T(8,128)(2,1)S(1)}, bf16[4,384,128]{2,1,0:T(8,128)(2,1)S(1)}, u32[]{:S(2)}, u32[]{:S(2)}) collective-permute-start(bf16[4,384,128]{2,1,0:T(8,128)(2,1)S(1)} %get-tuple-element.12), channel_id=1, source_target_pairs={{0,96},{96,0},{1,97},{97,1},{2,98},{98,2},{3,99},{99,3},{4,100},{1... | collective-permute-start | bytes 1179656 | tf_op jit(solution)/shard_map/ppermute | solution.py:204
